TPU v7x, 32 devices: a whole 2x2x4 slice. The times are simulated.
32 devices in a mesh: body: 16 (over z, x, core), row: 2 (over y).
Axes of the slice: x: 2, y: 2, z: 4, core: 2. Of those that a mesh axis runs over, the one named last changes fastest.
Arguments:
- strengths: bfloat16 [32, 131072], P(None, ('body', 'row')), may hold values from -6 to 6
- influence: bfloat16 [16, 2, 5, 32, 2, 128, 128], P('body', 'row'), may hold values from -0.09375 to 0.09375
- target_block: int32 [16, 2, 5, 32], P('body', 'row'), may hold values from 0 to 31
- source_block: int32 [16, 2, 5, 32], P('body', 'row'), may hold values from 0 to 63
- live_counts: int32 [16, 2, 5], P('body', 'row'), may hold values from 4 to 32, as said below
Outputs:
- response: float32 [32, 131072], P(None, ('body', 'row'))
Inputs may be any that keep to these rules, and one draw needn't show every extreme that they name: Slot k of a slice for source offset t is live when k < live_counts; for offset 2 (the group's own bodies) all 32 slots are live.
All inputs are finite; a program needn't handle non-finite values.
Results may differ from a plain program's by a relative error of at most 0.0003.
Values may be sent and summed in bfloat16 or wider, within the bound.
No kernel may reach another device: no remote copies, remote signals or barrier semaphores. Data moves between devices by JAX's collectives and lax.ppermute only.
A program may use at most 64 MiB of HBM per device.

v0:
```python
import jax
import jax.numpy as jnp
from jax import lax
from jax.sharding import PartitionSpec as P


def passed_along(array, axis, by):
    devices = lax.axis_size(axis)
    return lax.ppermute(array, axis, [(i, (i + by) % devices) for i in range(devices)])


def block_terms(slot_tiles, slot_rows, live_count, picked, row_blocks):
    channels = picked.shape[0]
    heads = channels // 2
    capacity = slot_tiles.shape[0]
    products = jnp.einsum("kprj,hkj->kphr", slot_tiles, picked, preferred_element_type=jnp.float32)
    real_part = products[:, 0, :heads] - products[:, 1, heads:]
    imag_part = products[:, 0, heads:] + products[:, 1, :heads]
    combined = jnp.concatenate([real_part, imag_part], axis=1)
    alive_mask = (jnp.arange(capacity, dtype=jnp.int32) < live_count).astype(jnp.float32)
    onehot = (slot_rows[:, None] == jnp.arange(row_blocks, dtype=jnp.int32)[None, :]).astype(
        jnp.float32
    )
    onehot = onehot * alive_mask[:, None]
    return jnp.einsum("kn,khr->hnr", onehot, combined, precision=lax.Precision.HIGHEST)


def pick_blocks(group_x, slot_cols, block_size):
    channels = group_x.shape[0]
    blocks = group_x.reshape(channels, -1, block_size)
    return jnp.take(blocks, slot_cols, axis=1)


def window(values, reach):
    windows = [(0, values)]
    for direction in (1, -1):
        current = values
        for hop_index in range(reach):
            current = passed_along(current, "body", direction)
            windows.append((-direction * (hop_index + 1), current))
    return windows


def on_device(strengths, influence, target_block, source_block, live_counts):
    channels, row_count = strengths.shape
    block_size = influence.shape[-1]
    row_blocks = row_count // block_size
    reach = (influence.shape[2] - 1) // 2
    totals = (0.5 * strengths.astype(jnp.float32)).reshape(channels, row_blocks, block_size)

    def apply_picked(totals_now, offset, picked):
        index = offset + reach
        return totals_now + block_terms(
            influence[0, 0, index],
            target_block[0, 0, index],
            live_counts[0, 0, index],
            picked,
            row_blocks,
        )

    def apply_offset(totals_now, offset, group_x):
        index = offset + reach
        picked = pick_blocks(group_x, source_block[0, 0, index], block_size)
        return apply_picked(totals_now, offset, picked)

    group_x = lax.all_gather(strengths, "row", axis=1, tiled=True)
    for offset, source_x in window(group_x, reach):
        totals = apply_offset(totals, offset, source_x)
    return totals.reshape(channels, row_count)


def solution(mesh):
    return jax.shard_map(
        on_device,
        mesh=mesh,
        in_specs=(
            P(None, ("body", "row")),
            P("body", "row", None, None, None, None, None),
            P("body", "row", None, None),
            P("body", "row", None, None),
            P("body", "row", None),
        ),
        out_specs=P(None, ("body", "row")),
        check_vma=False,
    )
```

profile of v0, /device:TPU:1, one launch (start us, length us, event | category | flops | bytes accessed | tf_op | source)
XLA Modules:
  0.0 56.6 jit_solution(6832906776811036869)
XLA Ops:
  0.0 9.0 %all_gather.3 = bf16[32,8192]{1,0:T(8,128)(2,1)S(1)} all-gather(bf16[32,4096]{1,0:T(8,128)(2,1)} %param.7), channel_id=1, replica_groups=mesh['body'=16,'row'=2] {'row'}, dimensions={1}, use_global_device_ids=true | all-gather | bytes 786432 | tf_op jit(solution)/shard_map/all_gather | solution.py:66
  9.0 2.5 %collective-permute-start = (bf16[32,8192]{1,0:T(8,128)(2,1)S(1)}, bf16[32,8192]{1,0:T(8,128)(2,1)S(1)}, u32[]{:S(2)}, u32[]{:S(2)}) collective-permute-start(bf16[32,8192]{1,0:T(8,128)(2,1)S(1)} %all_gather.3), channel_id=1, source_target_pairs={{0,2},{2,4},{4,6},{6,8},{8,10},{10,12},{12,14},{14,16},{16,18},{18... | collective-permute-start | bytes 1572872 | tf_op jit(solution)/shard_map/ppermute | solution.py:9
  11.5 0.0 collective-permute-start.2
  11.5 0.1 copy_bitcast_fusion.5
  11.6 1.0 %multiply_bitcast_fusion = f32[4,8,32,128]{3,1,2,0:T(8,128)S(1)} fusion(bf16[32,4096]{1,0:T(8,128)(2,1)} %param.7), kind=kLoop, calls=%fused_computation.51 | loop fusion | flops 262144 | bytes 786432
  12.6 0.7 %compare_and_fusion = (pred[32]{0:T(512)(128)(4,1)S(1)}, s32[32]{0:T(128)S(1)}, pred[32]{0:T(512)(128)(4,1)S(1)}, s32[32]{0:T(128)S(1)}, pred[32]{0:T(512)(128)(...) fusion(s32[1,1,5,32]{3,1,2,0:T(1,128)} %param.10), kind=kLoop, calls=%fused_computation.142 | loop fusion | flops 960 | bytes 1440 | tf_op jit(solution)/shard_map/jit(_take)/and | solution.py:31
  13.4 1.5 %fusion.110 = (s32[1,1,1]{2,1,0:T(1,128)}, s32[1,1,1]{2,1,0:T(1,128)}, s32[1,1,1]{2,1,0:T(1,128)}, s32[1,1,1]{2,1,0:T(1,128)}, s32[1,1,1]{2,1,0:T(1,128)}) fusion(s32[1,1,5]{2,1,0:T(1,128)} %param.11), kind=kLoop, calls=%fused_computation.167 | loop fusion | bytes 40 | tf_op jit(solution)/shard_map/slice | solution.py:56
  14.8 0.6 %compare_convert_fusion.2 = f32[32]{0:T(128)S(1)} fusion(s32[]{:T(128)} %bitcast.33), kind=kLoop, calls=%fused_computation.149 | loop fusion | flops 64 | bytes 132 | tf_op jit(solution)/shard_map/convert_element_type | solution.py:20
  15.4 0.6 %compare_convert_fusion.3 = f32[32]{0:T(128)S(1)} fusion(s32[]{:T(128)} %bitcast.21), kind=kLoop, calls=%fused_computation.150 | loop fusion | flops 64 | bytes 132 | tf_op jit(solution)/shard_map/convert_element_type | solution.py:20
  16.1 0.6 %compare_convert_fusion.1 = f32[32]{0:T(128)S(1)} fusion(s32[]{:T(128)} %bitcast.45), kind=kLoop, calls=%fused_computation.148 | loop fusion | flops 64 | bytes 132 | tf_op jit(solution)/shard_map/convert_element_type | solution.py:20
  16.7 0.6 %gather_fusion = bf16[32,32,128]{2,1,0:T(8,128)(2,1)S(1)} fusion(bf16[32,64,128]{2,0,1:T(8,128)(2,1)S(1)} %copy_bitcast_fusion.5, s32[1024]{0:T(1024)S(1)} %pad_clamp_fusion.4), kind=kCustom, calls=%fused_computation.clone | custom fusion | bytes 524416 | tf_op jit(solution)/shard_map/jit(_take)/gather | solution.py:31
  17.3 2.4 %fusion.15 = f32[32,2,32,128]{3,2,1,0:T(8,128)S(1)} fusion(bf16[1,1,5,32,2,128,128]{6,5,4,3,2,1,0:T(8,128)(2,1)} %param.8, bf16[32,32,128]{2,1,0:T(8,128)(2,1)S(1)} %gather_fusion, pred[32]{0:T(512)(128)(4,1)S(1)} %get-tuple-element.25), kind=kOutput, calls=%fused_computation.20 | convolution fusion | flops 67239936 | bytes 3407904 | tf_op jit(solution)/shard_map/kprj,hkj->kphr/dot_general | solution.py:16
  19.8 0.6 %compare_convert_fusion.4 = f32[32]{0:T(128)S(1)} fusion(s32[]{:T(128)} %bitcast.9), kind=kLoop, calls=%fused_computation.151 | loop fusion | flops 64 | bytes 132 | tf_op jit(solution)/shard_map/convert_element_type | solution.py:20
  20.4 0.1 copy.76
  20.6 0.7 %compare_convert_fusion = f32[32]{0:T(128)S(1)} fusion(s32[]{:T(128)} %bitcast.57), kind=kLoop, calls=%fused_computation.147 | loop fusion | flops 64 | bytes 132 | tf_op jit(solution)/shard_map/convert_element_type | solution.py:20
  21.3 0.1 pad_maximum_fusion
  21.3 0.7 %slice_bitcast_fusion.10 = (s32[32]{0:T(128)S(1)}, s32[32]{0:T(128)S(1)}, s32[32]{0:T(128)S(1)}, s32[32]{0:T(128)S(1)}, s32[32]{0:T(128)S(1)}) fusion(s32[1,1,5,32]{3,1,2,0:T(1,128)} %param.9), kind=kLoop, calls=%fused_computation.152 | loop fusion | bytes 1280 | tf_op jit(solution)/shard_map/eq | solution.py:21
  22.1 1.2 %collective-permute-done = bf16[32,8192]{1,0:T(8,128)(2,1)S(1)} collective-permute-done((bf16[32,8192]{1,0:T(8,128)(2,1)S(1)}, bf16[32,8192]{1,0:T(8,128)(2,1)S(1)}, u32[]{:S(2)}, u32[]{:S(2)}) %collective-permute-start) | collective-permute-done | bytes 524320 | tf_op jit(solution)/shard_map/ppermute | solution.py:9
  23.3 0.1 copy_bitcast_fusion.4
  23.4 0.6 %gather_fusion.1 = bf16[32,32,128]{2,1,0:T(8,128)(2,1)S(1)} fusion(bf16[32,64,128]{2,0,1:T(8,128)(2,1)S(1)} %copy_bitcast_fusion.4, s32[1024]{0:T(1024)S(1)} %pad_clamp_fusion.3), kind=kCustom, calls=%fused_computation.1.clone | custom fusion | bytes 524416 | tf_op jit(solution)/shard_map/jit(_take)/gather | solution.py:31
  24.0 2.4 %fusion.18 = f32[32,2,32,128]{3,2,1,0:T(8,128)S(1)} fusion(bf16[1,1,5,32,2,128,128]{6,5,4,3,2,1,0:T(8,128)(2,1)} %param.8, bf16[32,32,128]{2,1,0:T(8,128)(2,1)S(1)} %gather_fusion.1, pred[32]{0:T(512)(128)(4,1)S(1)} %get-tuple-element.23), kind=kOutput, calls=%fused_computation.21 | convolution fusion | flops 67239936 | bytes 3407904 | tf_op jit(solution)/shard_map/kprj,hkj->kphr/dot_general | solution.py:16
  26.5 0.0 collective-permute-done.2
  26.5 1.1 %copy_bitcast_fusion.2 = bf16[32,64,128]{2,0,1:T(8,128)(2,1)S(1)} fusion(bf16[32,8192]{1,0:T(8,128)(2,1)} %collective-permute-done.2), kind=kLoop, calls=%fused_computation.37 | loop fusion | bytes 1048576 | tf_op jit(solution)/shard_map/reshape | solution.py:30
  27.6 0.6 %gather_fusion.3 = bf16[32,32,128]{2,1,0:T(8,128)(2,1)S(1)} fusion(bf16[32,64,128]{2,0,1:T(8,128)(2,1)S(1)} %copy_bitcast_fusion.2, s32[1024]{0:T(1024)S(1)} %pad_clamp_fusion.1), kind=kCustom, calls=%fused_computation.3.clone | custom fusion | bytes 524416 | tf_op jit(solution)/shard_map/jit(_take)/gather | solution.py:31
  28.2 2.4 %fusion.24 = f32[32,2,32,128]{3,2,1,0:T(8,128)S(1)} fusion(bf16[1,1,5,32,2,128,128]{6,5,4,3,2,1,0:T(8,128)(2,1)} %param.8, bf16[32,32,128]{2,1,0:T(8,128)(2,1)S(1)} %gather_fusion.3, pred[32]{0:T(512)(128)(4,1)S(1)} %get-tuple-element.27), kind=kOutput, calls=%fused_computation.23 | convolution fusion | flops 67239936 | bytes 3407904 | tf_op jit(solution)/shard_map/kprj,hkj->kphr/dot_general | solution.py:16
  30.8 0.1 pad_maximum_fusion.1
  30.8 2.5 %collective-permute-start.1 = (bf16[32,8192]{1,0:T(8,128)(2,1)S(1)}, bf16[32,8192]{1,0:T(8,128)(2,1)S(1)}, u32[]{:S(2)}, u32[]{:S(2)}) collective-permute-start(bf16[32,8192]{1,0:T(8,128)(2,1)S(1)} %collective-permute-done), channel_id=1, source_target_pairs={{0,2},{2,4},{4,6},{6,8},{8,10},{10,12},{12,14},{14,16},{16,18},{18... | collective-permute-start | bytes 1572872 | tf_op jit(solution)/shard_map/ppermute | solution.py:9
  33.3 0.1 pad_maximum_fusion.3
  33.4 0.1 collective-permute-start.3
  33.5 0.9 %convolution_bitcast_fusion.3 = f32[32,32,128]{2,1,0:T(8,128)S(1)} fusion(f32[32,32,128]{2,1,0:T(8,128)S(1)} %pad_maximum_fusion.1, f32[32]{0:T(128)S(1)} %compare_convert_fusion.3, s32[32]{0:T(128)S(1)} %get-tuple-element.18), kind=kOutput, calls=%fused_computation.28 | convolution fusion | flops 50333696 | bytes 1048832 | tf_op jit(solution)/shard_map/kn,khr->hnr/dot_general | solution.py:25
  34.4 0.9 %convolution_bitcast_fusion.1 = f32[32,32,128]{2,1,0:T(8,128)S(1)} fusion(f32[32,32,128]{2,1,0:T(8,128)S(1)} %pad_maximum_fusion.3, f32[32]{0:T(128)S(1)} %compare_convert_fusion.1, s32[32]{0:T(128)S(1)} %get-tuple-element.20), kind=kOutput, calls=%fused_computation.26 | convolution fusion | flops 50333696 | bytes 1048832 | tf_op jit(solution)/shard_map/kn,khr->hnr/dot_general | solution.py:25
  35.3 9.8 %collective-permute-done.1 = bf16[32,8192]{1,0:T(8,128)(2,1)S(1)} collective-permute-done((bf16[32,8192]{1,0:T(8,128)(2,1)S(1)}, bf16[32,8192]{1,0:T(8,128)(2,1)S(1)}, u32[]{:S(2)}, u32[]{:S(2)}) %collective-permute-start.1) | collective-permute-done | bytes 524320 | tf_op jit(solution)/shard_map/ppermute | solution.py:9
  45.1 0.1 copy_bitcast_fusion.3
  45.2 0.6 %gather_fusion.2 = bf16[32,32,128]{2,1,0:T(8,128)(2,1)S(1)} fusion(bf16[32,64,128]{2,0,1:T(8,128)(2,1)S(1)} %copy_bitcast_fusion.3, s32[1024]{0:T(1024)S(1)} %pad_clamp_fusion.2), kind=kCustom, calls=%fused_computation.2.clone | custom fusion | bytes 524416 | tf_op jit(solution)/shard_map/jit(_take)/gather | solution.py:31
  45.8 2.4 %fusion.21 = f32[32,2,32,128]{3,2,1,0:T(8,128)S(1)} fusion(bf16[1,1,5,32,2,128,128]{6,5,4,3,2,1,0:T(8,128)(2,1)} %param.8, bf16[32,32,128]{2,1,0:T(8,128)(2,1)S(1)} %gather_fusion.2, pred[32]{0:T(512)(128)(4,1)S(1)} %get-tuple-element.21), kind=kOutput, calls=%fused_computation.22 | convolution fusion | flops 67239936 | bytes 3407904 | tf_op jit(solution)/shard_map/kprj,hkj->kphr/dot_general | solution.py:16
  48.3 0.0 collective-permute-done.3
  48.3 1.1 %copy_bitcast_fusion.1 = bf16[32,64,128]{2,0,1:T(8,128)(2,1)S(1)} fusion(bf16[32,8192]{1,0:T(8,128)(2,1)} %collective-permute-done.3), kind=kLoop, calls=%fused_computation.36 | loop fusion | bytes 1048576 | tf_op jit(solution)/shard_map/reshape | solution.py:30
  49.5 0.6 %gather_fusion.4 = bf16[32,32,128]{2,1,0:T(8,128)(2,1)S(1)} fusion(bf16[32,64,128]{2,0,1:T(8,128)(2,1)S(1)} %copy_bitcast_fusion.1, s32[1024]{0:T(1024)S(1)} %pad_clamp_fusion), kind=kCustom, calls=%fused_computation.4.clone | custom fusion | bytes 524416 | tf_op jit(solution)/shard_map/jit(_take)/gather | solution.py:31
  50.1 2.4 %fusion.27 = f32[32,2,32,128]{3,2,1,0:T(8,128)S(1)} fusion(bf16[1,1,5,32,2,128,128]{6,5,4,3,2,1,0:T(8,128)(2,1)} %param.8, bf16[32,32,128]{2,1,0:T(8,128)(2,1)S(1)} %gather_fusion.4, pred[32]{0:T(512)(128)(4,1)S(1)} %get-tuple-element.6), kind=kOutput, calls=%fused_computation.24 | convolution fusion | flops 67239936 | bytes 3407904 | tf_op jit(solution)/shard_map/kprj,hkj->kphr/dot_general | solution.py:16
  52.6 0.1 pad_maximum_fusion.2
  52.6 0.1 pad_maximum_fusion.4
  52.7 0.9 %convolution_bitcast_fusion.2 = f32[32,32,128]{2,1,0:T(8,128)S(1)} fusion(f32[32,32,128]{2,1,0:T(8,128)S(1)} %pad_maximum_fusion.2, f32[32]{0:T(128)S(1)} %compare_convert_fusion.2, s32[32]{0:T(128)S(1)} %get-tuple-element.17), kind=kOutput, calls=%fused_computation.27 | convolution fusion | flops 50333696 | bytes 1048832 | tf_op jit(solution)/shard_map/kn,khr->hnr/dot_general | solution.py:25
  53.6 1.0 %fusion.33 = f32[32,32,128]{2,1,0:T(8,128)S(1)} fusion(f32[32,32,128]{2,1,0:T(8,128)S(1)} %convolution_bitcast_fusion.1, f32[32,32,128]{2,1,0:T(8,128)S(1)} %convolution_bitcast_fusion.2, f32[32,32,128]{2,1,0:T(8,128)S(1)} %convolution_bitcast_fusion.3, f32[32,32,128]{2,1,0:T(8,128)S(1)} %bitcast.237, f32[32,32,128]{2,1,0:T(8,128)S(1)} %pad_maximum_fusion, ...), kind=kOutput, calls=%fused_computation.33 | convolution fusion | flops 50857984 | bytes 3145984 | tf_op jit(solution)/shard_map/kn,khr->hnr/dot_general | solution.py:25
  54.6 0.9 %fusion.34 = f32[32,32,128]{2,1,0:T(8,128)S(1)} fusion(f32[32,32,128]{2,1,0:T(8,128)S(1)} %fusion.33, f32[32,32,128]{2,1,0:T(8,128)S(1)} %pad_maximum_fusion.4, f32[32]{0:T(128)S(1)} %compare_convert_fusion, s32[32]{0:T(128)S(1)} %get-tuple-element.16), kind=kOutput, calls=%fused_computation.34 | convolution fusion | flops 50464768 | bytes 1573120 | tf_op jit(solution)/shard_map/kn,khr->hnr/dot_general | solution.py:25
  55.5 1.1 %copy.94 = f32[4,8,32,128]{3,1,2,0:T(8,128)} copy(f32[4,8,32,128]{3,2,1,0:T(8,128)S(1)} %bitcast.238) | data formatting | bytes 1048576
  (15 shorter events, 0.4 us)
Async XLA Ops:
  9.0 14.2 %collective-permute-start = (bf16[32,8192]{1,0:T(8,128)(2,1)S(1)}, bf16[32,8192]{1,0:T(8,128)(2,1)S(1)}, u32[]{:S(2)}, u32[]{:S(2)}) collective-permute-start(bf16[32,8192]{1,0:T(8,128)(2,1)S(1)} %all_gather.3), channel_id=1, source_target_pairs={{0,2},{2,4},{4,6},{6,8},{8,10},{10,12},{12,14},{14,16},{16,18},{18... | collective-permute-start | bytes 1572872 | tf_op jit(solution)/shard_map/ppermute | solution.py:9
  11.5 15.0 %collective-permute-start.2 = (bf16[32,8192]{1,0:T(8,128)(2,1)S(1)}, bf16[32,8192]{1,0:T(8,128)(2,1)}, u32[]{:S(2)}, u32[]{:S(2)}) collective-permute-start(bf16[32,8192]{1,0:T(8,128)(2,1)S(1)} %all_gather.3), channel_id=1, source_target_pairs={{0,30},{2,0},{4,2},{6,4},{8,6},{10,8},{12,10},{14,12},{16,14},{18,... | collective-permute-start | bytes 1572872 | tf_op jit(solution)/shard_map/ppermute | solution.py:9
  30.8 14.3 %collective-permute-start.1 = (bf16[32,8192]{1,0:T(8,128)(2,1)S(1)}, bf16[32,8192]{1,0:T(8,128)(2,1)S(1)}, u32[]{:S(2)}, u32[]{:S(2)}) collective-permute-start(bf16[32,8192]{1,0:T(8,128)(2,1)S(1)} %collective-permute-done), channel_id=1, source_target_pairs={{0,2},{2,4},{4,6},{6,8},{8,10},{10,12},{12,14},{14,16},{16,18},{18... | collective-permute-start | bytes 1572872 | tf_op jit(solution)/shard_map/ppermute | solution.py:9
  33.4 14.9 %collective-permute-start.3 = (bf16[32,8192]{1,0:T(8,128)(2,1)}, bf16[32,8192]{1,0:T(8,128)(2,1)}, u32[]{:S(2)}, u32[]{:S(2)}) collective-permute-start(bf16[32,8192]{1,0:T(8,128)(2,1)} %collective-permute-done.2), channel_id=1, source_target_pairs={{0,30},{2,0},{4,2},{6,4},{8,6},{10,8},{12,10},{14,12},{16,14},{18,... | collective-permute-start | bytes 1572872 | tf_op jit(solution)/shard_map/ppermute | solution.py:9
where the time goes:
time: 57.1 us; the launch traced here: 56.6 us
  matrix products  16.8 us (29%)
  waiting for transfers between devices  11 us (19%)
  blocking collectives  9.02 us (16%)
  local copies, waits for them, and re-layouts  8.95 us (16%)
  other arithmetic  5.46 us (10%)
  starting transfers between devices  5.1 us (9%)
    dot_general x5, matrix products, block_terms(): jnp.einsum('kprj,hkj->kphr', slot_tiles, picked, preferred_element_type=j...  12.2 us
    ppermute x4, waiting for transfers between devices, passed_along(): lax.ppermute(array, axis, [(i, (i + by) % devices) for i in range(devices)])  11 us
    all_gather x1, blocking collectives, on_device(): group_x = lax.all_gather(strengths, 'row', axis=1, tiled=True)  9.02 us
    ppermute x4, starting transfers between devices, passed_along(): lax.ppermute(array, axis, [(i, (i + by) % devices) for i in range(devices)])  5.1 us
    dot_general x5, matrix products, block_terms(): jnp.einsum('kn,khr->hnr', onehot, combined, precision=lax.Precision.HIGHEST)  4.6 us
    convert_element_type x5, other arithmetic, block_terms(): (jnp.arange(capacity, dtype=jnp.int32) < live_count).astype(jnp.float32)  3.1 us
    gather x5, local copies, waits for them, and re-layouts, pick_blocks(): return jnp.take(blocks, slot_cols, axis=1)  3.01 us
    reshape x5, local copies, waits for them, and re-layouts, pick_blocks(): blocks = group_x.reshape(channels, -1, block_size)  2.54 us
  transfers between devices with their start and end apart: 4, of which 2 were waited for; matrix products, arithmetic and copies ran while one was open for 33% of the time, Pallas kernels for 0%

commit v1 on v0

v1 whole, which is shorter than its diff:
```python
import functools

import jax
import jax.numpy as jnp
from jax import lax
from jax.experimental import pallas as pl
from jax.experimental.pallas import tpu as pltpu
from jax.sharding import PartitionSpec as P

AXES = ("body", "row")
UNROLL = 8


def send(array, move):
    bodies, rows = lax.axis_size("body"), lax.axis_size("row")
    pairs = []
    for body in range(bodies):
        for row in range(rows):
            to_body, to_row = move(body, row)
            pairs.append((body * rows + row, (to_body % bodies) * rows + to_row % rows))
    return lax.ppermute(array, AXES, pairs)


def slots_kernel(piece_of, block_size, x_ref, src_ref, infl_ref, tb_ref, sb_ref, live_ref, out_ref, buf, sems):
    offsets, capacity = infl_ref.shape[2:4]
    row_blocks = x_ref.shape[1] // block_size
    heads = x_ref.shape[0] // 2
    body, row = lax.axis_index("body"), lax.axis_index("row")

    def copy(t, b):
        span = pl.ds(b * UNROLL, UNROLL)
        return pltpu.make_async_copy(infl_ref.at[0, 0, t, span], buf.at[t, span], sems.at[t, b])

    def batches(t):
        return (live_ref[0, 0, t] + UNROLL - 1) // UNROLL

    def over(fn):
        def one(t, _):
            lax.fori_loop(0, batches(t), lambda b, c: (fn(t, b), c)[1], 0)
            return 0

        lax.fori_loop(0, offsets, one, 0)

    over(lambda t, b: copy(t, b).start())
    out_ref[...] = 0.5 * x_ref[...].astype(jnp.float32)

    def compute(t, b):
        copy(t, b).wait()
        live = live_ref[0, 0, t]
        products = []
        for i in range(UNROLL):
            k = b * UNROLL + i
            sb = sb_ref[0, 0, t, k]
            piece = piece_of(body, row, t, sb // row_blocks)
            column = pl.multiple_of((sb % row_blocks) * block_size, block_size)
            x = src_ref[piece, :, pl.ds(column, block_size)]
            x = jnp.where(k < live, x, jnp.zeros_like(x))
            turned = jnp.concatenate([-x[heads:], x[:heads]], axis=0)
            both = jnp.concatenate([x, turned], axis=1)
            tiles = jnp.concatenate([buf[t, k, 0], buf[t, k, 1]], axis=1)
            products.append(lax.dot_general(both, tiles, (((1,), (1,)), ((), ())), preferred_element_type=jnp.float32))
        for i in range(UNROLL):
            column = pl.multiple_of(tb_ref[0, 0, t, b * UNROLL + i] * block_size, block_size)
            out_ref[:, pl.ds(column, block_size)] += products[i]

    over(compute)


def apply_slots(x, src, influence, target_block, source_block, live_counts, piece_of):
    offsets, capacity = influence.shape[2:4]
    block_size = influence.shape[-1]
    smem = pl.BlockSpec(memory_space=pltpu.SMEM)
    vmem = pl.BlockSpec(memory_space=pltpu.VMEM)
    return pl.pallas_call(
        functools.partial(slots_kernel, piece_of, block_size),
        out_shape=jax.ShapeDtypeStruct(x.shape, jnp.float32),
        in_specs=[vmem, vmem, pl.BlockSpec(memory_space=pl.ANY), smem, smem, smem],
        out_specs=vmem,
        scratch_shapes=[
            pltpu.VMEM(influence.shape[2:], influence.dtype),
            pltpu.SemaphoreType.DMA((offsets, capacity // UNROLL)),
        ],
        compiler_params=pltpu.CompilerParams(vmem_limit_bytes=40 << 20),
        name="slots",
    )(x, src, influence, target_block, source_block, live_counts)


def paired_pieces(body, row, t, slot_slice):
    core, x = body % 2, (body // 2) % 2
    there = core + t - 2
    chip = (there + 2) // 2 - 1
    other_core = (there + 2) % 2 != core
    near = jnp.where(x == 0, 1, -1)
    place = jnp.where(chip == 0, 0, jnp.where(chip == near, 1, 2))
    return place * 2 + jnp.where(slot_slice == row, 0, 1) + jnp.where(other_core, 6, 0)


def paired_window(x):
    across_x = lambda body, row: (body ^ 2, row)
    across_y = lambda body, row: (body, 1 - row)
    along_z = lambda body, row: (body - 4 if body & 2 else body + 4, row)
    far_from_home = lambda body, row: ((body ^ 2) + 4 if body & 2 else (body ^ 2) - 4, row)
    other_core = lambda body, row: (body ^ 1, row)
    near = send(x, across_x)
    own_other = send(x, across_y)
    far = send(near, along_z)
    near_other = send(near, across_y)
    far_other = send(send(x, across_y), far_from_home)
    mine = jnp.stack([x, own_other, near, near_other, far, far_other])
    return jnp.concatenate([mine, send(mine, other_core)])


def plain_window(x, reach):
    rows = lax.axis_size("row")
    group = jnp.moveaxis(lax.all_gather(x, "row", axis=1, tiled=True).reshape(x.shape[0], rows, -1), 1, 0)
    shifted = lambda by: send(group, lambda body, row: (body - by, row))
    return jnp.concatenate([shifted(by) if by else group for by in range(-reach, reach + 1)])


def plain_pieces(rows, body, row, t, slot_slice):
    return t * rows + slot_slice


def on_device(strengths, influence, target_block, source_block, live_counts):
    bodies, rows = lax.axis_size("body"), lax.axis_size("row")
    reach = (influence.shape[2] - 1) // 2
    if rows == 2 and reach == 2 and bodies % 4 == 0 and bodies >= 8:
        src, piece_of = paired_window(strengths), paired_pieces
    else:
        src, piece_of = plain_window(strengths, reach), functools.partial(plain_pieces, rows)
    return apply_slots(strengths, src, influence, target_block, source_block, live_counts, piece_of)


def solution(mesh):
    return jax.shard_map(
        on_device,
        mesh=mesh,
        in_specs=(
            P(None, ("body", "row")),
            P("body", "row", None, None, None, None, None),
            P("body", "row", None, None),
            P("body", "row", None, None),
            P("body", "row", None),
        ),
        out_specs=P(None, ("body", "row")),
        check_vma=False,
    )
```

time: 57.1 us -> 40.6 us (0.71)
  the two profiles are of different devices: /device:TPU:1 before, /device:TPU:9 now
where the time goes in v1:
time: 40.6 us; the launch traced here: 40.4 us
  waiting for transfers between devices  17.6 us (43%)
  starting transfers between devices  10.2 us (25%)
  Pallas kernels  7.2 us (18%)
  local copies, waits for them, and re-layouts  5.31 us (13%)
    ppermute x6, waiting for transfers between devices, send(): return lax.ppermute(array, AXES, pairs)  17.6 us
    ppermute x6, starting transfers between devices, send(): return lax.ppermute(array, AXES, pairs)  10.2 us
    pallas_call x1, Pallas kernels, apply_slots(): pl.pallas_call(functools.partial(slots_kernel, piece_of, block_size), out...  7.2 us
    unnamed x17, local copies, waits for them, and re-layouts  5.18 us
  transfers between devices with their start and end apart: 6, of which 4 were waited for; matrix products, arithmetic and copies ran while one was open for 3% of the time, Pallas kernels for 0%

profile of v1, /device:TPU:9, one launch (start us, length us, event | category | flops | bytes accessed | tf_op | source)
XLA Modules:
  0.0 40.4 jit_solution(11197926516638995312)
XLA Ops:
  0.0 0.0 copy-start.3
  0.0 0.0 copy-start.4
  0.0 1.2 %collective-permute-start = (bf16[32,4096]{1,0:T(8,128)(2,1)}, bf16[32,4096]{1,0:T(8,128)(2,1)S(1)}, u32[]{:S(2)}, u32[]{:S(2)}) collective-permute-start(bf16[32,4096]{1,0:T(8,128)(2,1)} %x_ref.1), channel_id=1, source_target_pairs={{0,1},{1,0},{2,3},{3,2},{4,5},{5,4},{6,7},{7,6},{8,9},{9,8},{10,11... | collective-permute-start | bytes 786440 | tf_op jit(solution)/shard_map/ppermute | solution.py:21
  1.2 1.2 %collective-permute-start.1 = (bf16[32,4096]{1,0:T(8,128)(2,1)}, bf16[32,4096]{1,0:T(8,128)(2,1)S(1)}, u32[]{:S(2)}, u32[]{:S(2)}) collective-permute-start(bf16[32,4096]{1,0:T(8,128)(2,1)} %x_ref.1), channel_id=1, source_target_pairs={{0,4},{1,5},{2,6},{3,7},{4,0},{5,1},{6,2},{7,3},{8,12},{9,13},{10,... | collective-permute-start | bytes 786440 | tf_op jit(solution)/shard_map/ppermute | solution.py:21
  2.5 1.0 %bitcast_dynamic-update-slice_fusion.11 = (bf16[6,32,4096]{2,1,0:T(8,128)(2,1)S(1)}, bf16[12,32,4096]{2,1,0:T(8,128)(2,1)S(1)}) fusion(bf16[32,4096]{1,0:T(8,128)(2,1)} %x_ref.1), kind=kLoop, calls=%fused_computation.11 | loop fusion | bytes 786432
  3.5 4.8 %collective-permute-done.1 = bf16[32,4096]{1,0:T(8,128)(2,1)S(1)} collective-permute-done((bf16[32,4096]{1,0:T(8,128)(2,1)}, bf16[32,4096]{1,0:T(8,128)(2,1)S(1)}, u32[]{:S(2)}, u32[]{:S(2)}) %collective-permute-start.1) | collective-permute-done | bytes 262176 | tf_op jit(solution)/shard_map/ppermute | solution.py:21
  8.3 0.2 collective-permute-start.2
  8.5 1.3 %collective-permute-start.3 = (bf16[32,4096]{1,0:T(8,128)(2,1)S(1)}, bf16[32,4096]{1,0:T(8,128)(2,1)S(1)}, u32[]{:S(2)}, u32[]{:S(2)}) collective-permute-start(bf16[32,4096]{1,0:T(8,128)(2,1)S(1)} %collective-permute-done.1), channel_id=1, source_target_pairs={{0,8},{1,9},{2,10},{3,11},{4,28},{5,29},{6,30},{7,31},{8,16},{9,17... | collective-permute-start | bytes 786440 | tf_op jit(solution)/shard_map/ppermute | solution.py:21
  9.8 0.0 collective-permute-done
  9.8 3.1 %collective-permute-start.4 = (bf16[32,4096]{1,0:T(8,128)(2,1)S(1)}, bf16[32,4096]{1,0:T(8,128)(2,1)S(1)}, u32[]{:S(2)}, u32[]{:S(2)}) collective-permute-start(bf16[32,4096]{1,0:T(8,128)(2,1)S(1)} %collective-permute-done), channel_id=1, source_target_pairs={{0,28},{1,29},{2,30},{3,31},{4,8},{5,9},{6,10},{7,11},{8,4},{9,5},... | collective-permute-start | bytes 786440 | tf_op jit(solution)/shard_map/ppermute | solution.py:21
  13.0 0.0 copy-start.1
  13.0 0.0 copy-start.2
  13.1 1.2 %collective-permute-done.2 = bf16[32,4096]{1,0:T(8,128)(2,1)S(1)} collective-permute-done((bf16[32,4096]{1,0:T(8,128)(2,1)S(1)}, bf16[32,4096]{1,0:T(8,128)(2,1)S(1)}, u32[]{:S(2)}, u32[]{:S(2)}) %collective-permute-start.2) | collective-permute-done | bytes 262176 | tf_op jit(solution)/shard_map/ppermute | solution.py:21
  14.3 0.0 collective-permute-done.3
  14.3 8.5 %collective-permute-done.4 = bf16[32,4096]{1,0:T(8,128)(2,1)S(1)} collective-permute-done((bf16[32,4096]{1,0:T(8,128)(2,1)S(1)}, bf16[32,4096]{1,0:T(8,128)(2,1)S(1)}, u32[]{:S(2)}, u32[]{:S(2)}) %collective-permute-start.4) | collective-permute-done | bytes 262176 | tf_op jit(solution)/shard_map/ppermute | solution.py:21
  22.9 3.1 %collective-permute-start.5 = (bf16[6,32,4096]{2,1,0:T(8,128)(2,1)S(1)}, bf16[6,32,4096]{2,1,0:T(8,128)(2,1)S(1)}, u32[]{:S(2)}, u32[]{:S(2)}) collective-permute-start(bf16[6,32,4096]{2,1,0:T(8,128)(2,1)S(1)} %get-tuple-element.5), channel_id=1, source_target_pairs={{0,2},{1,3},{2,0},{3,1},{4,6},{5,7},{6,4},{7,5},{8,10},{9,11},{10,... | collective-permute-start | bytes 4718600 | tf_op jit(solution)/shard_map/ppermute | solution.py:21
  26.0 0.0 copy-done.3
  26.0 0.0 copy-done.4
  26.0 3.0 %collective-permute-done.5 = bf16[6,32,4096]{2,1,0:T(8,128)(2,1)S(1)} collective-permute-done((bf16[6,32,4096]{2,1,0:T(8,128)(2,1)S(1)}, bf16[6,32,4096]{2,1,0:T(8,128)(2,1)S(1)}, u32[]{:S(2)}, u32[]{:S(2)}) %collective-permute-start.5) | collective-permute-done | bytes 1572896 | tf_op jit(solution)/shard_map/ppermute | solution.py:21
  29.0 0.1 constant_dynamic-update-slice_fusion.src_ref
  29.1 0.0 copy-done.1
  29.1 0.0 copy-done.2
  29.1 0.0 copy-start
  29.2 4.0 %copy-done = bf16[1,1,5,32,2,128,128]{6,5,4,3,2,1,0:T(8,128)(2,1)S(1)} copy-done((bf16[1,1,5,32,2,128,128]{6,5,4,3,2,1,0:T(8,128)(2,1)S(1)}, bf16[1,1,5,32,2,128,128]{6,5,4,3,2,1,0:T(8,128)(2,1)}, u32[]{:S(2)}) %copy-start) | copy-done | bytes 10485784
  33.1 7.2 %slots.1 = f32[32,4096]{1,0:T(8,128)} custom-call(bf16[32,4096]{1,0:T(8,128)(2,1)S(1)} %copy-done.1, bf16[12,32,4096]{2,1,0:T(8,128)(2,1)S(1)} %constant_dynamic-update-slice_fusion.src_ref, bf16[1,1,5,32,2,128,128]{6,5,4,3,2,1,0:T(8,128)(2,1)S(1)} %copy-done, s32[1,1,5,32]{3,2,1,0:T(8,128)S(1)} %copy.6.tb_ref, s32[1,1,5,32]{3,2,1,0:T(8,128)S(1)} %copy.7.sb_ref, ...), custom_call_target="tpu_custom_call" | custom-call | tf_op jit(solution)/shard_map/slots/pallas_call | solution.py:74
  (7 shorter events, 0.2 us)
Async XLA Ops:
  0.0 26.0 %copy-start.3 = (s32[1,1,5,32]{3,1,2,0:T(1,128)S(1)}, s32[1,1,5,32]{3,1,2,0:T(1,128)}, u32[]{:S(2)}) copy-start(s32[1,1,5,32]{3,1,2,0:T(1,128)} %param.7) | copy-start | bytes 1924
  0.0 26.0 %copy-start.4 = (s32[1,1,5,32]{3,1,2,0:T(1,128)S(1)}, s32[1,1,5,32]{3,1,2,0:T(1,128)}, u32[]{:S(2)}) copy-start(s32[1,1,5,32]{3,1,2,0:T(1,128)} %param.8) | copy-start | bytes 1924
  0.0 9.8 %collective-permute-start = (bf16[32,4096]{1,0:T(8,128)(2,1)}, bf16[32,4096]{1,0:T(8,128)(2,1)S(1)}, u32[]{:S(2)}, u32[]{:S(2)}) collective-permute-start(bf16[32,4096]{1,0:T(8,128)(2,1)} %x_ref.1), channel_id=1, source_target_pairs={{0,1},{1,0},{2,3},{3,2},{4,5},{5,4},{6,7},{7,6},{8,9},{9,8},{10,11... | collective-permute-start | bytes 786440 | tf_op jit(solution)/shard_map/ppermute | solution.py:21
  1.2 7.1 %collective-permute-start.1 = (bf16[32,4096]{1,0:T(8,128)(2,1)}, bf16[32,4096]{1,0:T(8,128)(2,1)S(1)}, u32[]{:S(2)}, u32[]{:S(2)}) collective-permute-start(bf16[32,4096]{1,0:T(8,128)(2,1)} %x_ref.1), channel_id=1, source_target_pairs={{0,4},{1,5},{2,6},{3,7},{4,0},{5,1},{6,2},{7,3},{8,12},{9,13},{10,... | collective-permute-start | bytes 786440 | tf_op jit(solution)/shard_map/ppermute | solution.py:21
  8.3 5.9 %collective-permute-start.2 = (bf16[32,4096]{1,0:T(8,128)(2,1)S(1)}, bf16[32,4096]{1,0:T(8,128)(2,1)S(1)}, u32[]{:S(2)}, u32[]{:S(2)}) collective-permute-start(bf16[32,4096]{1,0:T(8,128)(2,1)S(1)} %collective-permute-done.1), channel_id=1, source_target_pairs={{0,1},{1,0},{2,3},{3,2},{4,5},{5,4},{6,7},{7,6},{8,9},{9,8},{10,11... | collective-permute-start | bytes 786440 | tf_op jit(solution)/shard_map/ppermute | solution.py:21
  8.5 5.7 %collective-permute-start.3 = (bf16[32,4096]{1,0:T(8,128)(2,1)S(1)}, bf16[32,4096]{1,0:T(8,128)(2,1)S(1)}, u32[]{:S(2)}, u32[]{:S(2)}) collective-permute-start(bf16[32,4096]{1,0:T(8,128)(2,1)S(1)} %collective-permute-done.1), channel_id=1, source_target_pairs={{0,8},{1,9},{2,10},{3,11},{4,28},{5,29},{6,30},{7,31},{8,16},{9,17... | collective-permute-start | bytes 786440 | tf_op jit(solution)/shard_map/ppermute | solution.py:21
  9.8 13.0 %collective-permute-start.4 = (bf16[32,4096]{1,0:T(8,128)(2,1)S(1)}, bf16[32,4096]{1,0:T(8,128)(2,1)S(1)}, u32[]{:S(2)}, u32[]{:S(2)}) collective-permute-start(bf16[32,4096]{1,0:T(8,128)(2,1)S(1)} %collective-permute-done), channel_id=1, source_target_pairs={{0,28},{1,29},{2,30},{3,31},{4,8},{5,9},{6,10},{7,11},{8,4},{9,5},... | collective-permute-start | bytes 786440 | tf_op jit(solution)/shard_map/ppermute | solution.py:21
  13.0 16.1 %copy-start.1 = (bf16[32,4096]{1,0:T(8,128)(2,1)S(1)}, bf16[32,4096]{1,0:T(8,128)(2,1)}, u32[]{:S(2)}) copy-start(bf16[32,4096]{1,0:T(8,128)(2,1)} %x_ref.1) | copy-start | bytes 786436
  13.0 16.1 %copy-start.2 = (s32[1,1,5]{2,1,0:T(1,128)S(1)}, s32[1,1,5]{2,1,0:T(1,128)}, u32[]{:S(2)}) copy-start(s32[1,1,5]{2,1,0:T(1,128)} %live_ref.1) | copy-start | bytes 64
  22.9 6.1 %collective-permute-start.5 = (bf16[6,32,4096]{2,1,0:T(8,128)(2,1)S(1)}, bf16[6,32,4096]{2,1,0:T(8,128)(2,1)S(1)}, u32[]{:S(2)}, u32[]{:S(2)}) collective-permute-start(bf16[6,32,4096]{2,1,0:T(8,128)(2,1)S(1)} %get-tuple-element.5), channel_id=1, source_target_pairs={{0,2},{1,3},{2,0},{3,1},{4,6},{5,7},{6,4},{7,5},{8,10},{9,11},{10,... | collective-permute-start | bytes 4718600 | tf_op jit(solution)/shard_map/ppermute | solution.py:21
  29.1 4.0 %copy-start = (bf16[1,1,5,32,2,128,128]{6,5,4,3,2,1,0:T(8,128)(2,1)S(1)}, bf16[1,1,5,32,2,128,128]{6,5,4,3,2,1,0:T(8,128)(2,1)}, u32[]{:S(2)}) copy-start(bf16[1,1,5,32,2,128,128]{6,5,4,3,2,1,0:T(8,128)(2,1)} %infl_ref.1) | copy-start | bytes 31457284

commit v2 on v1

v2 whole, which is shorter than its diff:
```python
import functools

import jax
import jax.numpy as jnp
from jax import lax
from jax.experimental import pallas as pl
from jax.experimental.pallas import tpu as pltpu
from jax.sharding import PartitionSpec as P

AXES = ("body", "row")
UNROLL = 8
SMEM = pl.BlockSpec(memory_space=pltpu.SMEM)
VMEM = pl.BlockSpec(memory_space=pltpu.VMEM)


def send(array, move):
    bodies, rows = lax.axis_size("body"), lax.axis_size("row")
    pairs = []
    for body in range(bodies):
        for row in range(rows):
            to_body, to_row = move(body, row)
            pairs.append((body * rows + row, (to_body % bodies) * rows + to_row % rows))
    return lax.ppermute(array, AXES, pairs)


def live_batches(live_ref, t):
    return (live_ref[0, 0, t] + UNROLL - 1) // UNROLL


def over_batches(live_ref, offsets, wanted, fn):
    def one(t, carry):
        batches = jnp.where(wanted(t), live_batches(live_ref, t), 0)
        lax.fori_loop(0, batches, lambda b, c: (fn(t, b), c)[1], 0)
        return carry

    lax.fori_loop(0, offsets, one, 0)


def fetch_kernel(infl_ref, live_ref, kept_ref, sems):
    def copy(t, b):
        span = pl.ds(b * UNROLL, UNROLL)
        return pltpu.make_async_copy(infl_ref.at[0, 0, t, span], kept_ref.at[t, span], sems.at[t, b])

    everywhere = functools.partial(over_batches, live_ref, kept_ref.shape[0], lambda t: True)
    everywhere(lambda t, b: copy(t, b).start())
    everywhere(lambda t, b: copy(t, b).wait())


def fetch(influence, live_counts):
    offsets, capacity = influence.shape[2:4]
    return pl.pallas_call(
        fetch_kernel,
        out_shape=jax.ShapeDtypeStruct(influence.shape[2:], influence.dtype),
        in_specs=[pl.BlockSpec(memory_space=pltpu.HBM), SMEM],
        out_specs=pl.BlockSpec(memory_space=pl.ANY),
        scratch_shapes=[pltpu.SemaphoreType.DMA((offsets, capacity // UNROLL))],
        compiler_params=pltpu.CompilerParams(vmem_limit_bytes=4 << 20),
        cost_estimate=pl.CostEstimate(flops=0, transcendentals=0, bytes_accessed=influence.size * 4),
        name="fetch",
    )(pltpu.with_memory_space_constraint(influence, pltpu.HBM), live_counts)


def slots_kernel(piece_of, scale, start_ref, src_ref, kept_ref, tb_ref, sb_ref, live_ref, out_ref):
    offsets, block_size = kept_ref.shape[0], kept_ref.shape[-1]
    row_blocks = start_ref.shape[1] // block_size
    heads = start_ref.shape[0] // 2
    pieces = src_ref.shape[0]
    body, row = lax.axis_index("body"), lax.axis_index("row")
    start = start_ref[...].astype(jnp.float32)
    out_ref[...] = start if scale == 1 else scale * start

    def wanted(t):
        piece = piece_of(body, row, t, 0)
        return (piece >= 0) & (piece < pieces)

    def compute(t, b):
        live = live_ref[0, 0, t]
        products = []
        for i in range(UNROLL):
            k = b * UNROLL + i
            sb = sb_ref[0, 0, t, k]
            piece = piece_of(body, row, t, sb // row_blocks)
            column = pl.multiple_of((sb % row_blocks) * block_size, block_size)
            x = src_ref[piece, :, pl.ds(column, block_size)]
            x = jnp.where(k < live, x, jnp.zeros_like(x))
            turned = jnp.concatenate([-x[heads:], x[:heads]], axis=0)
            both = jnp.concatenate([x, turned], axis=1)
            tiles = jnp.concatenate([kept_ref[t, k, 0], kept_ref[t, k, 1]], axis=1)
            products.append(lax.dot_general(both, tiles, (((1,), (1,)), ((), ())), preferred_element_type=jnp.float32))
        for i in range(UNROLL):
            column = pl.multiple_of(tb_ref[0, 0, t, b * UNROLL + i] * block_size, block_size)
            out_ref[:, pl.ds(column, block_size)] += products[i]

    over_batches(live_ref, offsets, wanted, compute)


def add_slots(start, scale, src, kept, target_block, source_block, live_counts, piece_of, name):
    return pl.pallas_call(
        functools.partial(slots_kernel, piece_of, scale),
        out_shape=jax.ShapeDtypeStruct(start.shape, jnp.float32),
        in_specs=[VMEM, VMEM, VMEM, SMEM, SMEM, SMEM],
        out_specs=VMEM,
        compiler_params=pltpu.CompilerParams(vmem_limit_bytes=4 << 20),
        cost_estimate=pl.CostEstimate(flops=0, transcendentals=0, bytes_accessed=8 << 20),
        name=name,
    )(start, src, kept, target_block, source_block, live_counts)


def chip_of(body, t):
    core, x = body % 2, (body // 2) % 2
    there = core + t - 2
    chip = (there + 2) // 2 - 1
    other_core = ((there + 2) % 2 != core).astype(jnp.int32)
    near = jnp.where(x == 0, 1, -1)
    return jnp.where(chip == 0, 0, jnp.where(chip == near, 1, 2)), other_core


def early_pieces(body, row, t, slot_slice):
    place, other_core = chip_of(body, t)
    piece = other_core * 4 + place * 2 + jnp.where(slot_slice == row, 0, 1)
    return jnp.where(place == 2, -1, piece)


def late_pieces(body, row, t, slot_slice):
    place, other_core = chip_of(body, t)
    piece = other_core * 2 + jnp.where(slot_slice == row, 0, 1)
    return jnp.where(place == 2, piece, -1)


def across_x(body, row):
    return body ^ 2, row


def across_y(body, row):
    return body, 1 - row


def along_z(body, row):
    return (body - 4 if body & 2 else body + 4), row


def to_far_chip(body, row):
    return ((body ^ 2) + 4 if body & 2 else (body ^ 2) - 4), row


def other_core(body, row):
    return body ^ 1, row


def paired(x, influence, *slots):
    kept = fetch(influence, slots[2])
    near = send(x, across_x)
    own_other = send(x, across_y)
    far = send(near, along_z)
    far_other = send(own_other, to_far_chip)
    near_other = send(near, across_y)
    early = jnp.stack([x, own_other, near, near_other])
    early = jnp.concatenate([early, send(early, other_core)])
    half = add_slots(x, 0.5, early, kept, *slots, early_pieces, "early_slots")
    far, far_other, half = lax.optimization_barrier((far, far_other, half))
    late = jnp.stack([far, far_other])
    late = jnp.concatenate([late, send(late, other_core)])
    return add_slots(half, 1, late, kept, *slots, late_pieces, "late_slots")


def plain_pieces(rows, body, row, t, slot_slice):
    return t * rows + slot_slice


def plain(x, influence, *slots):
    rows, reach = lax.axis_size("row"), (influence.shape[2] - 1) // 2
    group = jnp.moveaxis(lax.all_gather(x, "row", axis=1, tiled=True).reshape(x.shape[0], rows, -1), 1, 0)
    shifted = lambda by: send(group, lambda body, row: (body - by, row))
    src = jnp.concatenate([shifted(by) if by else group for by in range(-reach, reach + 1)])
    return add_slots(x, 0.5, src, fetch(influence, slots[2]), *slots, functools.partial(plain_pieces, rows), "slots")


def on_device(strengths, influence, target_block, source_block, live_counts):
    bodies, rows = lax.axis_size("body"), lax.axis_size("row")
    on_chips = rows == 2 and influence.shape[2] == 5 and bodies % 4 == 0 and bodies >= 8
    return (paired if on_chips else plain)(strengths, influence, target_block, source_block, live_counts)


def solution(mesh):
    return jax.shard_map(
        on_device,
        mesh=mesh,
        in_specs=(
            P(None, ("body", "row")),
            P("body", "row", None, None, None, None, None),
            P("body", "row", None, None),
            P("body", "row", None, None),
            P("body", "row", None),
        ),
        out_specs=P(None, ("body", "row")),
        check_vma=False,
    )
```

time: 40.6 us -> 32.1 us (0.79)
  the two profiles are of different devices: /device:TPU:9 before, /device:TPU:0 now
where the time goes in v2:
time: 32.1 us; the launch traced here: 31.6 us
  starting transfers between devices  10.1 us (31%)
  waiting for transfers between devices  9.29 us (29%)
  Pallas kernels  8.65 us (27%)
  local copies, waits for them, and re-layouts  3.16 us (10%)
    ppermute x7, starting transfers between devices, send(): return lax.ppermute(array, AXES, pairs)  10.1 us
    ppermute x7, waiting for transfers between devices, send(): return lax.ppermute(array, AXES, pairs)  9.29 us
    pallas_call x2, Pallas kernels, add_slots(): pl.pallas_call(functools.partial(slots_kernel, piece_of, scale), out_shap...  5.43 us
    pallas_call x1, Pallas kernels, fetch(): pl.pallas_call(fetch_kernel, out_shape=jax.ShapeDtypeStruct(influence.sha...  3.23 us
    unnamed x10, local copies, waits for them, and re-layouts  3.09 us
  transfers between devices with their start and end apart: 7, of which 5 were waited for; matrix products, arithmetic and copies ran while one was open for 8% of the time, Pallas kernels for 19%

profile of v2, /device:TPU:0, one launch (start us, length us, event | category | flops | bytes accessed | tf_op | source)
XLA Modules:
  0.0 31.6 jit_solution(10516358490921200115)
XLA Ops:
  0.0 3.0 %collective-permute-start.2 = (bf16[32,4096]{1,0:T(8,128)(2,1)}, bf16[32,4096]{1,0:T(8,128)(2,1)S(1)}, u32[]{:S(2)}, u32[]{:S(2)}) collective-permute-start(bf16[32,4096]{1,0:T(8,128)(2,1)} %start_ref.1), channel_id=1, source_target_pairs={{0,1},{1,0},{2,3},{3,2},{4,5},{5,4},{6,7},{7,6},{8,9},{9,8},{10,11... | collective-permute-start | bytes 786440 | tf_op jit(solution)/shard_map/ppermute | solution.py:23
  3.0 1.5 %collective-permute-start = (bf16[32,4096]{1,0:T(8,128)(2,1)}, bf16[32,4096]{1,0:T(8,128)(2,1)S(1)}, u32[]{:S(2)}, u32[]{:S(2)}) collective-permute-start(bf16[32,4096]{1,0:T(8,128)(2,1)} %start_ref.1), channel_id=1, source_target_pairs={{0,4},{1,5},{2,6},{3,7},{4,0},{5,1},{6,2},{7,3},{8,12},{9,13},{10,... | collective-permute-start | bytes 786440 | tf_op jit(solution)/shard_map/ppermute | solution.py:23
  4.5 1.0 %constant_dynamic-update-slice_fusion.4 = bf16[8,32,4096]{2,1,0:T(8,128)(2,1)S(1)} fusion(bf16[32,4096]{1,0:T(8,128)(2,1)} %start_ref.1), kind=kLoop, calls=%fused_computation.7 | loop fusion | bytes 524288
  5.5 0.7 %copy.6.tb_ref = s32[1,1,5,32]{3,2,1,0:T(8,128)S(1)} copy(s32[1,1,5,32]{3,1,2,0:T(1,128)} %param.7) | data formatting | bytes 1280 | tf_op args[2]
  6.2 0.7 %copy.7.sb_ref = s32[1,1,5,32]{3,2,1,0:T(8,128)S(1)} copy(s32[1,1,5,32]{3,1,2,0:T(1,128)} %param.8) | data formatting | bytes 1280 | tf_op args[3]
  6.8 0.0 copy-start.1
  6.8 0.7 %copy-done.1 = s32[1,1,5]{2,1,0:T(1,128)S(1)} copy-done((s32[1,1,5]{2,1,0:T(1,128)S(1)}, s32[1,1,5]{2,1,0:T(1,128)}, u32[]{:S(2)}) %copy-start.1) | copy-done | bytes 44
  7.5 0.0 copy-start
  7.5 3.2 %fetch.1.kept_ref = bf16[5,32,2,128,128]{4,3,2,1,0:T(8,128)(2,1)S(1)} custom-call(bf16[1,1,5,32,2,128,128]{6,5,4,3,2,1,0:T(8,128)(2,1)} %infl_ref.1, s32[1,1,5]{2,1,0:T(1,128)S(1)} %copy-done.1), custom_call_target="tpu_custom_call" | custom-call | bytes 20971520 | tf_op jit(solution)/shard_map/fetch/pallas_call | solution.py:51
  10.7 0.2 collective-permute-done
  10.9 0.7 %collective-permute-start.4 = (bf16[32,4096]{1,0:T(8,128)(2,1)S(1)}, bf16[32,4096]{1,0:T(8,128)(2,1)S(1)}, u32[]{:S(2)}, u32[]{:S(2)}) collective-permute-start(bf16[32,4096]{1,0:T(8,128)(2,1)S(1)} %collective-permute-done), channel_id=1, source_target_pairs={{0,1},{1,0},{2,3},{3,2},{4,5},{5,4},{6,7},{7,6},{8,9},{9,8},{10,11... | collective-permute-start | bytes 786440 | tf_op jit(solution)/shard_map/ppermute | solution.py:23
  11.6 1.7 %collective-permute-start.1 = (bf16[32,4096]{1,0:T(8,128)(2,1)S(1)}, bf16[32,4096]{1,0:T(8,128)(2,1)S(1)}, u32[]{:S(2)}, u32[]{:S(2)}) collective-permute-start(bf16[32,4096]{1,0:T(8,128)(2,1)S(1)} %collective-permute-done), channel_id=1, source_target_pairs={{0,8},{1,9},{2,10},{3,11},{4,28},{5,29},{6,30},{7,31},{8,16},{9,17... | collective-permute-start | bytes 786440 | tf_op jit(solution)/shard_map/ppermute | solution.py:23
  13.4 0.0 collective-permute-done.2
  13.4 3.1 %collective-permute-start.3 = (bf16[32,4096]{1,0:T(8,128)(2,1)S(1)}, bf16[32,4096]{1,0:T(8,128)(2,1)S(1)}, u32[]{:S(2)}, u32[]{:S(2)}) collective-permute-start(bf16[32,4096]{1,0:T(8,128)(2,1)S(1)} %collective-permute-done.2), channel_id=1, source_target_pairs={{0,28},{1,29},{2,30},{3,31},{4,8},{5,9},{6,10},{7,11},{8,4},{9,5},... | collective-permute-start | bytes 786440 | tf_op jit(solution)/shard_map/ppermute | solution.py:23
  16.5 1.7 %collective-permute-done.4 = bf16[32,4096]{1,0:T(8,128)(2,1)S(1)} collective-permute-done((bf16[32,4096]{1,0:T(8,128)(2,1)S(1)}, bf16[32,4096]{1,0:T(8,128)(2,1)S(1)}, u32[]{:S(2)}, u32[]{:S(2)}) %collective-permute-start.4) | collective-permute-done | bytes 262176 | tf_op jit(solution)/shard_map/ppermute | solution.py:23
  18.1 0.0 copy-done
  18.1 0.1 pad_maximum_fusion
  18.3 0.1 collective-permute-start.5
  18.4 2.6 %collective-permute-done.5 = bf16[4,32,4096]{2,1,0:T(8,128)(2,1)S(1)} collective-permute-done((bf16[4,32,4096]{2,1,0:T(8,128)(2,1)S(1)}, bf16[4,32,4096]{2,1,0:T(8,128)(2,1)S(1)}, u32[]{:S(2)}, u32[]{:S(2)}) %collective-permute-start.5) | collective-permute-done | bytes 1048608 | tf_op jit(solution)/shard_map/ppermute | solution.py:23
  21.0 0.1 constant_dynamic-update-slice_fusion.src_ref
  21.1 2.9 %early_slots.1.start_ref = f32[32,4096]{1,0:T(8,128)S(1)} custom-call(bf16[32,4096]{1,0:T(8,128)(2,1)S(1)} %copy-done, bf16[8,32,4096]{2,1,0:T(8,128)(2,1)S(1)} %constant_dynamic-update-slice_fusion.src_ref, bf16[5,32,2,128,128]{4,3,2,1,0:T(8,128)(2,1)S(1)} %fetch.1.kept_ref, s32[1,1,5,32]{3,2,1,0:T(8,128)S(1)} %copy.6.tb_ref, ...), custom_call_target="tpu_custom_call" | custom-call | bytes 8388608 | tf_op jit(solution)/shard_map/early_slots/pallas_call | solution.py:98
  24.0 2.9 %collective-permute-done.3 = bf16[32,4096]{1,0:T(8,128)(2,1)S(1)} collective-permute-done((bf16[32,4096]{1,0:T(8,128)(2,1)S(1)}, bf16[32,4096]{1,0:T(8,128)(2,1)S(1)}, u32[]{:S(2)}, u32[]{:S(2)}) %collective-permute-start.3) | collective-permute-done | bytes 262176 | tf_op jit(solution)/shard_map/ppermute | solution.py:23
  26.9 0.0 collective-permute-done.1
  26.9 0.1 pad_maximum_fusion.2
  26.9 0.1 collective-permute-start.6
  27.0 1.9 %collective-permute-done.6 = bf16[2,32,4096]{2,1,0:T(8,128)(2,1)S(1)} collective-permute-done((bf16[2,32,4096]{2,1,0:T(8,128)(2,1)S(1)}, bf16[2,32,4096]{2,1,0:T(8,128)(2,1)S(1)}, u32[]{:S(2)}, u32[]{:S(2)}) %collective-permute-start.6) | collective-permute-done | bytes 524320 | tf_op jit(solution)/shard_map/ppermute | solution.py:23
  28.9 0.1 pad_maximum_fusion.1.src_ref
  29.0 2.5 %late_slots.1 = f32[32,4096]{1,0:T(8,128)} custom-call(f32[32,4096]{1,0:T(8,128)S(1)} %early_slots.1.start_ref, bf16[4,32,4096]{2,1,0:T(8,128)(2,1)S(1)} %pad_maximum_fusion.1.src_ref, bf16[5,32,2,128,128]{4,3,2,1,0:T(8,128)(2,1)S(1)} %fetch.1.kept_ref, s32[1,1,5,32]{3,2,1,0:T(8,128)S(1)} %copy.6.tb_ref, s32[1,1,5,32]{3,2,1,0:T(8,128)S(1)} %copy.7.sb_ref, ...), custom_call_target="tpu_custom_call" | custom-call | bytes 8388608 | tf_op jit(solution)/shard_map/late_slots/pallas_call | solution.py:98
  (3 shorter events, 0.1 us)
Async XLA Ops:
  0.0 13.4 %collective-permute-start.2 = (bf16[32,4096]{1,0:T(8,128)(2,1)}, bf16[32,4096]{1,0:T(8,128)(2,1)S(1)}, u32[]{:S(2)}, u32[]{:S(2)}) collective-permute-start(bf16[32,4096]{1,0:T(8,128)(2,1)} %start_ref.1), channel_id=1, source_target_pairs={{0,1},{1,0},{2,3},{3,2},{4,5},{5,4},{6,7},{7,6},{8,9},{9,8},{10,11... | collective-permute-start | bytes 786440 | tf_op jit(solution)/shard_map/ppermute | solution.py:23
  3.0 8.0 %collective-permute-start = (bf16[32,4096]{1,0:T(8,128)(2,1)}, bf16[32,4096]{1,0:T(8,128)(2,1)S(1)}, u32[]{:S(2)}, u32[]{:S(2)}) collective-permute-start(bf16[32,4096]{1,0:T(8,128)(2,1)} %start_ref.1), channel_id=1, source_target_pairs={{0,4},{1,5},{2,6},{3,7},{4,0},{5,1},{6,2},{7,3},{8,12},{9,13},{10,... | collective-permute-start | bytes 786440 | tf_op jit(solution)/shard_map/ppermute | solution.py:23
  6.8 0.7 %copy-start.1 = (s32[1,1,5]{2,1,0:T(1,128)S(1)}, s32[1,1,5]{2,1,0:T(1,128)}, u32[]{:S(2)}) copy-start(s32[1,1,5]{2,1,0:T(1,128)} %live_ref.5) | copy-start | bytes 64
  7.5 10.6 %copy-start = (bf16[32,4096]{1,0:T(8,128)(2,1)S(1)}, bf16[32,4096]{1,0:T(8,128)(2,1)}, u32[]{:S(2)}) copy-start(bf16[32,4096]{1,0:T(8,128)(2,1)} %start_ref.1) | copy-start | bytes 786436
  10.9 7.2 %collective-permute-start.4 = (bf16[32,4096]{1,0:T(8,128)(2,1)S(1)}, bf16[32,4096]{1,0:T(8,128)(2,1)S(1)}, u32[]{:S(2)}, u32[]{:S(2)}) collective-permute-start(bf16[32,4096]{1,0:T(8,128)(2,1)S(1)} %collective-permute-done), channel_id=1, source_target_pairs={{0,1},{1,0},{2,3},{3,2},{4,5},{5,4},{6,7},{7,6},{8,9},{9,8},{10,11... | collective-permute-start | bytes 786440 | tf_op jit(solution)/shard_map/ppermute | solution.py:23
  11.6 15.3 %collective-permute-start.1 = (bf16[32,4096]{1,0:T(8,128)(2,1)S(1)}, bf16[32,4096]{1,0:T(8,128)(2,1)S(1)}, u32[]{:S(2)}, u32[]{:S(2)}) collective-permute-start(bf16[32,4096]{1,0:T(8,128)(2,1)S(1)} %collective-permute-done), channel_id=1, source_target_pairs={{0,8},{1,9},{2,10},{3,11},{4,28},{5,29},{6,30},{7,31},{8,16},{9,17... | collective-permute-start | bytes 786440 | tf_op jit(solution)/shard_map/ppermute | solution.py:23
  13.4 13.5 %collective-permute-start.3 = (bf16[32,4096]{1,0:T(8,128)(2,1)S(1)}, bf16[32,4096]{1,0:T(8,128)(2,1)S(1)}, u32[]{:S(2)}, u32[]{:S(2)}) collective-permute-start(bf16[32,4096]{1,0:T(8,128)(2,1)S(1)} %collective-permute-done.2), channel_id=1, source_target_pairs={{0,28},{1,29},{2,30},{3,31},{4,8},{5,9},{6,10},{7,11},{8,4},{9,5},... | collective-permute-start | bytes 786440 | tf_op jit(solution)/shard_map/ppermute | solution.py:23
  18.3 2.7 %collective-permute-start.5 = (bf16[4,32,4096]{2,1,0:T(8,128)(2,1)S(1)}, bf16[4,32,4096]{2,1,0:T(8,128)(2,1)S(1)}, u32[]{:S(2)}, u32[]{:S(2)}) collective-permute-start(bf16[4,32,4096]{2,1,0:T(8,128)(2,1)S(1)} %pad_maximum_fusion), channel_id=1, source_target_pairs={{0,2},{1,3},{2,0},{3,1},{4,6},{5,7},{6,4},{7,5},{8,10},{9,11},{10,... | collective-permute-start | bytes 3145736 | tf_op jit(solution)/shard_map/ppermute | solution.py:23
  26.9 2.0 %collective-permute-start.6 = (bf16[2,32,4096]{2,1,0:T(8,128)(2,1)S(1)}, bf16[2,32,4096]{2,1,0:T(8,128)(2,1)S(1)}, u32[]{:S(2)}, u32[]{:S(2)}) collective-permute-start(bf16[2,32,4096]{2,1,0:T(8,128)(2,1)S(1)} %pad_maximum_fusion.2), channel_id=1, source_target_pairs={{0,2},{1,3},{2,0},{3,1},{4,6},{5,7},{6,4},{7,5},{8,10},{9,11},{10,... | collective-permute-start | bytes 1572872 | tf_op jit(solution)/shard_map/ppermute | solution.py:23

commit v3 on v1

v3 whole, which is shorter than its diff:
```python
import functools

import jax
import jax.numpy as jnp
from jax import lax
from jax.experimental import pallas as pl
from jax.experimental.pallas import tpu as pltpu
from jax.sharding import PartitionSpec as P

AXES = ("body", "row")
UNROLL = 8
SMEM = pl.BlockSpec(memory_space=pltpu.SMEM)
VMEM = pl.BlockSpec(memory_space=pltpu.VMEM)


def send(array, move):
    bodies, rows = lax.axis_size("body"), lax.axis_size("row")
    pairs = []
    for body in range(bodies):
        for row in range(rows):
            to_body, to_row = move(body, row)
            pairs.append((body * rows + row, (to_body % bodies) * rows + to_row % rows))
    return lax.ppermute(array, AXES, pairs)


def prepare_kernel(route, stages, row_blocks, infl_ref, *refs):
    *small_refs, kept_ref, list_ref, tb_ref, sb_ref, live_ref, sems, small_sems = refs
    offsets, capacity = kept_ref.shape[:2]
    body, row = lax.axis_index("body"), lax.axis_index("row")
    last = list_ref.shape[1] - 1
    tb_copy, sb_copy, live_copy = (
        pltpu.make_async_copy(hbm, smem, small_sems.at[i])
        for i, (hbm, smem) in enumerate(zip(small_refs, (tb_ref, sb_ref, live_ref)))
    )
    live_copy.start()
    tb_copy.start()
    sb_copy.start()
    live_copy.wait()

    def each_copy(act):
        def one(t, carry):
            def batch(b, c):
                span = pl.ds(b * UNROLL, UNROLL)
                act(pltpu.make_async_copy(infl_ref.at[0, 0, t, span], kept_ref.at[t, span], sems.at[t, b]))
                return c

            return lax.fori_loop(0, (live_ref[0, 0, t] + UNROLL - 1) // UNROLL, batch, carry)

        lax.fori_loop(0, offsets, one, 0)

    each_copy(lambda copy: copy.start())
    tb_copy.wait()
    sb_copy.wait()

    def one(t, counts):
        def slot(k, counts):
            sb = sb_ref[t, 0, k]
            stage, place = route(body, row, t, sb // row_blocks, sb % row_blocks)
            at = counts[0]
            for s in range(1, stages):
                at = jnp.where(stage == s, counts[s], at)
            list_ref[stage, at] = ((t * capacity + k) << 18) + (place << 6) + tb_ref[t, 0, k]
            return tuple(counts[s] + jnp.where(stage == s, 1, 0) for s in range(stages))

        return lax.fori_loop(0, live_ref[0, 0, t], slot, counts)

    counts = lax.fori_loop(0, offsets, one, (jnp.int32(0),) * stages)
    for s in range(stages):
        for i in range(UNROLL - 1):
            list_ref[s, counts[s] + i] = 0
        list_ref[s, last] = counts[s]
    each_copy(lambda copy: copy.wait())


def prepare(influence, target_block, source_block, live_counts, route, stages, row_blocks):
    offsets, capacity = influence.shape[2:4]
    in_hbm = lambda a: pltpu.with_memory_space_constraint(a, pltpu.HBM)
    by_offset = lambda a: in_hbm(jnp.transpose(a, (0, 2, 1, 3)).reshape(offsets, 1, capacity))
    hbm = pl.BlockSpec(memory_space=pltpu.HBM)
    return pl.pallas_call(
        functools.partial(prepare_kernel, route, stages, row_blocks),
        out_shape=(
            jax.ShapeDtypeStruct(influence.shape[2:], influence.dtype),
            jax.ShapeDtypeStruct((stages, offsets * capacity + UNROLL), jnp.int32),
        ),
        in_specs=[hbm] * 4,
        out_specs=(pl.BlockSpec(memory_space=pl.ANY), SMEM),
        scratch_shapes=[
            pltpu.SMEM((offsets, 1, capacity), jnp.int32),
            pltpu.SMEM((offsets, 1, capacity), jnp.int32),
            pltpu.SMEM(live_counts.shape, jnp.int32),
            pltpu.SemaphoreType.DMA((offsets, capacity // UNROLL)),
            pltpu.SemaphoreType.DMA((3,)),
        ],
        compiler_params=pltpu.CompilerParams(vmem_limit_bytes=4 << 20),
        cost_estimate=pl.CostEstimate(flops=0, transcendentals=0, bytes_accessed=1024),
        name="prepare",
    )(in_hbm(influence), by_offset(target_block), by_offset(source_block), in_hbm(live_counts))


def slots_kernel(stage, *refs):
    *totals, src_ref, kept_ref, list_ref, out_ref = refs
    block_size, capacity = kept_ref.shape[-1], kept_ref.shape[1]
    piece_blocks = src_ref.shape[2] // block_size
    heads = src_ref.shape[1] // 2
    out_ref[...] = totals[0][...] if totals else 0.5 * src_ref[0].astype(jnp.float32)
    count = list_ref[stage, list_ref.shape[1] - 1]

    def compute(b, carry):
        products, columns = [], []
        for i in range(UNROLL):
            entry = list_ref[stage, b * UNROLL + i]
            slot, place, target = entry >> 18, (entry >> 6) & 4095, entry & 63
            column = pl.multiple_of((place % piece_blocks) * block_size, block_size)
            x = src_ref[place // piece_blocks, :, pl.ds(column, block_size)]
            x = jnp.where(b * UNROLL + i < count, x, jnp.zeros_like(x))
            turned = jnp.concatenate([-x[heads:], x[:heads]], axis=0)
            both = jnp.concatenate([x, turned], axis=1)
            t, k = slot // capacity, slot % capacity
            tiles = jnp.concatenate([kept_ref[t, k, 0], kept_ref[t, k, 1]], axis=1)
            products.append(lax.dot_general(both, tiles, (((1,), (1,)), ((), ())), preferred_element_type=jnp.float32))
            columns.append(pl.multiple_of(target * block_size, block_size))
        for product, column in zip(products, columns):
            out_ref[:, pl.ds(column, block_size)] += product
        return carry

    lax.fori_loop(0, (count + UNROLL - 1) // UNROLL, compute, 0)


def add_slots(totals, src, kept, lists, stage, name):
    return pl.pallas_call(
        functools.partial(slots_kernel, stage),
        out_shape=jax.ShapeDtypeStruct(src.shape[1:], jnp.float32),
        in_specs=[VMEM] * len(totals) + [VMEM, VMEM, SMEM],
        out_specs=VMEM,
        compiler_params=pltpu.CompilerParams(vmem_limit_bytes=4 << 20),
        cost_estimate=pl.CostEstimate(flops=0, transcendentals=0, bytes_accessed=1024),
        name=name,
    )(*totals, src, kept, lists)


EARLY, MIDDLE, LATE = range(3)


def chip_route(row_blocks, body, row, t, slot_slice, block):
    core, x = body % 2, (body // 2) % 2
    there = core + t - 2
    chip = (there + 2) // 2 - 1
    crossed = ((there + 2) % 2 != core).astype(jnp.int32)
    other_row = (slot_slice != row).astype(jnp.int32)
    own, near = chip == 0, chip == jnp.where(x == 0, 1, -1)
    both = crossed + other_row
    stage = jnp.where(own, both // 2, jnp.where(near, jnp.minimum(1 + both, LATE), both))
    own_piece = jnp.where(crossed == 0, other_row, 3 - other_row)
    near_piece = jnp.where(both == 0, 0, 2 * crossed - other_row * crossed)
    far_piece = jnp.where(both == 0, 2, jnp.where(both == 2, 3, 1 + 2 * crossed))
    piece = jnp.where(own, own_piece, jnp.where(near, near_piece, far_piece))
    return stage, piece * row_blocks + block


def across_x(body, row):
    return body ^ 2, row


def across_y(body, row):
    return body, 1 - row


def to_far_chip(body, row):
    return ((body ^ 2) + 4 if body & 2 else (body ^ 2) - 4), row


def other_core(body, row):
    return body ^ 1, row


def after(value, *earlier):
    return lax.optimization_barrier((value, *earlier))[0]


def both_cores(*pieces):
    mine = jnp.stack(pieces) if len(pieces) > 1 else pieces[0][None]
    return jnp.concatenate([mine, send(mine, other_core)])


def by_chips(x, influence, target_block, source_block, live_counts):
    row_blocks = x.shape[1] // influence.shape[-1]
    kept, lists = prepare(
        influence, target_block, source_block, live_counts, functools.partial(chip_route, row_blocks), 3, row_blocks
    )
    half = x.shape[1] // 2
    half = x.shape[1] // 2
    far = send(x, to_far_chip)
    near = send(x, across_x)
    own_other = send(x, across_y)
    crossed_x = send(x, other_core)
    far, own_other, kept, lists = lax.optimization_barrier((far, own_other, kept, lists))
    far_other = send(far, across_y)
    near_other = send(own_other, across_x)
    crossed = [send(piece, other_core) for piece in (own_other, far)]
    total = add_slots([], jnp.stack([x, own_other, far, crossed_x]), kept, lists, EARLY, "early_slots")
    middle = jnp.stack([after(near, total), far_other, *crossed])
    total = add_slots([total], middle, kept, lists, MIDDLE, "middle_slots")
    late = jnp.stack([after(near_other, total), near, far_other])
    late = jnp.concatenate([late[:1], send(late, other_core)])
    return add_slots([total], late, kept, lists, LATE, "late_slots")


def plain_route(rows, row_blocks, body, row, t, slot_slice, block):
    return 0, (1 + t * rows + slot_slice) * row_blocks + block


def plain(x, influence, target_block, source_block, live_counts):
    rows, reach = lax.axis_size("row"), (influence.shape[2] - 1) // 2
    row_blocks = x.shape[1] // influence.shape[-1]
    route = functools.partial(plain_route, rows, row_blocks)
    kept, lists = prepare(influence, target_block, source_block, live_counts, route, 1, row_blocks)
    group = jnp.moveaxis(lax.all_gather(x, "row", axis=1, tiled=True).reshape(x.shape[0], rows, -1), 1, 0)
    shifted = lambda by: send(group, lambda body, row: (body - by, row))
    src = jnp.concatenate([x[None]] + [shifted(by) if by else group for by in range(-reach, reach + 1)])
    return add_slots([], src, kept, lists, 0, "slots")


def on_device(strengths, influence, target_block, source_block, live_counts):
    bodies, rows = lax.axis_size("body"), lax.axis_size("row")
    on_chips = rows == 2 and influence.shape[2] == 5 and bodies % 4 == 0 and bodies >= 8
    return (by_chips if on_chips else plain)(strengths, influence, target_block, source_block, live_counts)


def solution(mesh):
    return jax.shard_map(
        on_device,
        mesh=mesh,
        in_specs=(
            P(None, ("body", "row")),
            P("body", "row", None, None, None, None, None),
            P("body", "row", None, None),
            P("body", "row", None, None),
            P("body", "row", None),
        ),
        out_specs=P(None, ("body", "row")),
        check_vma=False,
    )
```

time: 40.6 us -> 30.4 us (0.75)
  the two profiles are of different devices: /device:TPU:9 before, /device:TPU:1 now
where the time goes in v3:
time: 30.4 us
  Pallas kernels  14.7 us (48%)
  starting transfers between devices  11 us (36%)
  waiting for transfers between devices  4.26 us (14%)
  other arithmetic  0.45 us (1%)
    ppermute x9, starting transfers between devices, send(): return lax.ppermute(array, AXES, pairs)  11 us
    pallas_call x1, Pallas kernels, prepare(): pl.pallas_call(functools.partial(prepare_kernel, route, stages, row_block...  7.38 us
    pallas_call x3, Pallas kernels, add_slots(): pl.pallas_call(functools.partial(slots_kernel, stage), out_shape=jax.Shap...  7.28 us
    ppermute x9, waiting for transfers between devices, send(): return lax.ppermute(array, AXES, pairs)  4.26 us
  transfers between devices with their start and end apart: 9, of which 2 were waited for; matrix products, arithmetic and copies ran while one was open for 1% of the time, Pallas kernels for 40%

profile of v3, /device:TPU:1, one launch (start us, length us, event | category | flops | bytes accessed | tf_op | source)
XLA Modules:
  0.0 30.4 jit_solution(8144886120095676459)
XLA Ops:
  0.0 0.0 copy-start
  0.0 5.1 %collective-permute-start = (bf16[32,4096]{1,0:T(8,128)(2,1)}, bf16[32,4096]{1,0:T(8,128)(2,1)S(1)}, u32[]{:S(2)}, u32[]{:S(2)}) collective-permute-start(bf16[32,4096]{1,0:T(8,128)(2,1)} %param.5), channel_id=1, source_target_pairs={{0,28},{1,29},{2,30},{3,31},{4,8},{5,9},{6,10},{7,11},{8,4},{9,5},... | collective-permute-start | bytes 786440 | tf_op jit(solution)/shard_map/ppermute | solution.py:23
  5.1 1.2 %collective-permute-start.1 = (bf16[32,4096]{1,0:T(8,128)(2,1)}, bf16[32,4096]{1,0:T(8,128)(2,1)S(1)}, u32[]{:S(2)}, u32[]{:S(2)}) collective-permute-start(bf16[32,4096]{1,0:T(8,128)(2,1)} %param.5), channel_id=1, source_target_pairs={{0,1},{1,0},{2,3},{3,2},{4,5},{5,4},{6,7},{7,6},{8,9},{9,8},{10,11... | collective-permute-start | bytes 786440 | tf_op jit(solution)/shard_map/ppermute | solution.py:23
  6.3 1.2 %collective-permute-start.2 = (bf16[32,4096]{1,0:T(8,128)(2,1)}, bf16[32,4096]{1,0:T(8,128)(2,1)S(1)}, u32[]{:S(2)}, u32[]{:S(2)}) collective-permute-start(bf16[32,4096]{1,0:T(8,128)(2,1)} %param.5), channel_id=1, source_target_pairs={{0,2},{1,3},{2,0},{3,1},{4,6},{5,7},{6,4},{7,5},{8,10},{9,11},{10,... | collective-permute-start | bytes 786440 | tf_op jit(solution)/shard_map/ppermute | solution.py:23
  7.6 0.0 collective-permute-start.3
  7.6 7.4 %prepare.1 = (bf16[5,32,2,128,128]{4,3,2,1,0:T(8,128)(2,1)S(1)}, s32[3,168]{1,0:T(4,128)S(1)}) custom-call(bf16[1,1,5,32,2,128,128]{6,5,4,3,2,1,0:T(8,128)(2,1)} %infl_ref.1, s32[5,1,32]{2,1,0:T(1,128)} %bitcast.24, s32[5,1,32]{2,1,0:T(1,128)} %bitcast.25, s32[1,1,5]{2,1,0:T(1,128)} %refs_2_.1), custom_call_target="tpu_custom_call" | custom-call | bytes 1024 | tf_op jit(solution)/shard_map/prepare/pallas_call | solution.py:80
  14.9 0.0 collective-permute-done
  15.0 0.0 collective-permute-done.1
  15.0 0.5 %collective-permute-start.4 = (bf16[32,4096]{1,0:T(8,128)(2,1)S(1)}, bf16[32,4096]{1,0:T(8,128)(2,1)S(1)}, u32[]{:S(2)}, u32[]{:S(2)}) collective-permute-start(bf16[32,4096]{1,0:T(8,128)(2,1)S(1)} %collective-permute-done), channel_id=1, source_target_pairs={{0,1},{1,0},{2,3},{3,2},{4,5},{5,4},{6,7},{7,6},{8,9},{9,8},{10,11... | collective-permute-start | bytes 786440 | tf_op jit(solution)/shard_map/ppermute | solution.py:23
  15.4 0.1 collective-permute-start.6
  15.5 0.4 %collective-permute-start.5 = (bf16[32,4096]{1,0:T(8,128)(2,1)S(1)}, bf16[32,4096]{1,0:T(8,128)(2,1)S(1)}, u32[]{:S(2)}, u32[]{:S(2)}) collective-permute-start(bf16[32,4096]{1,0:T(8,128)(2,1)S(1)} %collective-permute-done.1), channel_id=1, source_target_pairs={{0,2},{1,3},{2,0},{3,1},{4,6},{5,7},{6,4},{7,5},{8,10},{9,11},{10,... | collective-permute-start | bytes 786440 | tf_op jit(solution)/shard_map/ppermute | solution.py:23
  16.0 0.0 collective-permute-done.2
  16.0 2.2 %collective-permute-start.7 = (bf16[32,4096]{1,0:T(8,128)(2,1)S(1)}, bf16[32,4096]{1,0:T(8,128)(2,1)S(1)}, u32[]{:S(2)}, u32[]{:S(2)}) collective-permute-start(bf16[32,4096]{1,0:T(8,128)(2,1)S(1)} %collective-permute-done.1), channel_id=1, source_target_pairs={{0,4},{1,5},{2,6},{3,7},{4,0},{5,1},{6,2},{7,3},{8,12},{9,13},{10,... | collective-permute-start | bytes 786440 | tf_op jit(solution)/shard_map/ppermute | solution.py:23
  18.2 0.0 copy-done
  18.2 0.1 pad_maximum_fusion.refs_0_
  18.3 2.3 %early_slots.1.refs_0_ = f32[32,4096]{1,0:T(8,128)S(1)} custom-call(bf16[4,32,4096]{2,1,0:T(8,128)(2,1)S(1)} %pad_maximum_fusion.refs_0_, bf16[5,32,2,128,128]{4,3,2,1,0:T(8,128)(2,1)S(1)} %get-tuple-element.17.refs_1_.refs_2_, s32[3,168]{1,0:T(4,128)S(1)} %get-tuple-element.18.refs_2_.refs_3_), custom_call_target="tpu_custom_call" | custom-call | bytes 1024 | tf_op jit(solution)/shard_map/early_slots/pallas_call | solution.py:131
  20.7 0.0 collective-permute-done.3
  20.7 2.1 %collective-permute-done.4 = bf16[32,4096]{1,0:T(8,128)(2,1)S(1)} collective-permute-done((bf16[32,4096]{1,0:T(8,128)(2,1)S(1)}, bf16[32,4096]{1,0:T(8,128)(2,1)S(1)}, u32[]{:S(2)}, u32[]{:S(2)}) %collective-permute-start.4) | collective-permute-done | bytes 262176 | tf_op jit(solution)/shard_map/ppermute | solution.py:23
  22.8 0.0 collective-permute-done.5
  22.8 0.0 collective-permute-done.6
  22.8 0.1 pad_maximum_fusion.1.refs_1_
  22.9 2.3 %middle_slots.1.refs_0_ = f32[32,4096]{1,0:T(8,128)S(1)} custom-call(f32[32,4096]{1,0:T(8,128)S(1)} %early_slots.1.refs_0_, bf16[4,32,4096]{2,1,0:T(8,128)(2,1)S(1)} %pad_maximum_fusion.1.refs_1_, bf16[5,32,2,128,128]{4,3,2,1,0:T(8,128)(2,1)S(1)} %get-tuple-element.17.refs_1_.refs_2_, s32[3,168]{1,0:T(4,128)S(1)} %get-tuple-element.18.refs_2_.refs_3_), custom_call_target="tpu_custom_call" | custom-call | bytes 1024 | tf_op jit(solution)/shard_map/middle_slots/pallas_call | solution.py:131
  25.3 0.0 collective-permute-done.7
  25.3 0.1 pad_maximum_fusion.3
  25.4 0.2 collective-permute-start.8
  25.6 2.1 %collective-permute-done.8 = bf16[3,32,4096]{2,1,0:T(8,128)(2,1)S(1)} collective-permute-done((bf16[3,32,4096]{2,1,0:T(8,128)(2,1)S(1)}, bf16[3,32,4096]{2,1,0:T(8,128)(2,1)S(1)}, u32[]{:S(2)}, u32[]{:S(2)}) %collective-permute-start.8) | collective-permute-done | bytes 786464 | tf_op jit(solution)/shard_map/ppermute | solution.py:23
  27.8 0.1 pad_maximum_fusion.2.refs_1_
  27.9 2.6 %late_slots.1 = f32[32,4096]{1,0:T(8,128)} custom-call(f32[32,4096]{1,0:T(8,128)S(1)} %middle_slots.1.refs_0_, bf16[4,32,4096]{2,1,0:T(8,128)(2,1)S(1)} %pad_maximum_fusion.2.refs_1_, bf16[5,32,2,128,128]{4,3,2,1,0:T(8,128)(2,1)S(1)} %get-tuple-element.17.refs_1_.refs_2_, s32[3,168]{1,0:T(4,128)S(1)} %get-tuple-element.18.refs_2_.refs_3_), custom_call_target="tpu_custom_call" | custom-call | bytes 1024 | tf_op jit(solution)/shard_map/late_slots/pallas_call | solution.py:131
Async XLA Ops:
  0.0 18.2 %copy-start = (bf16[32,4096]{1,0:T(8,128)(2,1)S(1)}, bf16[32,4096]{1,0:T(8,128)(2,1)}, u32[]{:S(2)}) copy-start(bf16[32,4096]{1,0:T(8,128)(2,1)} %param.5) | copy-start | bytes 786436
  0.0 14.9 %collective-permute-start = (bf16[32,4096]{1,0:T(8,128)(2,1)}, bf16[32,4096]{1,0:T(8,128)(2,1)S(1)}, u32[]{:S(2)}, u32[]{:S(2)}) collective-permute-start(bf16[32,4096]{1,0:T(8,128)(2,1)} %param.5), channel_id=1, source_target_pairs={{0,28},{1,29},{2,30},{3,31},{4,8},{5,9},{6,10},{7,11},{8,4},{9,5},... | collective-permute-start | bytes 786440 | tf_op jit(solution)/shard_map/ppermute | solution.py:23
  5.1 9.9 %collective-permute-start.1 = (bf16[32,4096]{1,0:T(8,128)(2,1)}, bf16[32,4096]{1,0:T(8,128)(2,1)S(1)}, u32[]{:S(2)}, u32[]{:S(2)}) collective-permute-start(bf16[32,4096]{1,0:T(8,128)(2,1)} %param.5), channel_id=1, source_target_pairs={{0,1},{1,0},{2,3},{3,2},{4,5},{5,4},{6,7},{7,6},{8,9},{9,8},{10,11... | collective-permute-start | bytes 786440 | tf_op jit(solution)/shard_map/ppermute | solution.py:23
  6.3 9.6 %collective-permute-start.2 = (bf16[32,4096]{1,0:T(8,128)(2,1)}, bf16[32,4096]{1,0:T(8,128)(2,1)S(1)}, u32[]{:S(2)}, u32[]{:S(2)}) collective-permute-start(bf16[32,4096]{1,0:T(8,128)(2,1)} %param.5), channel_id=1, source_target_pairs={{0,2},{1,3},{2,0},{3,1},{4,6},{5,7},{6,4},{7,5},{8,10},{9,11},{10,... | collective-permute-start | bytes 786440 | tf_op jit(solution)/shard_map/ppermute | solution.py:23
  7.6 13.1 %collective-permute-start.3 = (bf16[32,4096]{1,0:T(8,128)(2,1)}, bf16[32,4096]{1,0:T(8,128)(2,1)S(1)}, u32[]{:S(2)}, u32[]{:S(2)}) collective-permute-start(bf16[32,4096]{1,0:T(8,128)(2,1)} %param.5), channel_id=1, source_target_pairs={{0,4},{1,5},{2,6},{3,7},{4,0},{5,1},{6,2},{7,3},{8,12},{9,13},{10,... | collective-permute-start | bytes 786440 | tf_op jit(solution)/shard_map/ppermute | solution.py:23
  15.0 7.8 %collective-permute-start.4 = (bf16[32,4096]{1,0:T(8,128)(2,1)S(1)}, bf16[32,4096]{1,0:T(8,128)(2,1)S(1)}, u32[]{:S(2)}, u32[]{:S(2)}) collective-permute-start(bf16[32,4096]{1,0:T(8,128)(2,1)S(1)} %collective-permute-done), channel_id=1, source_target_pairs={{0,1},{1,0},{2,3},{3,2},{4,5},{5,4},{6,7},{7,6},{8,9},{9,8},{10,11... | collective-permute-start | bytes 786440 | tf_op jit(solution)/shard_map/ppermute | solution.py:23
  15.4 7.4 %collective-permute-start.6 = (bf16[32,4096]{1,0:T(8,128)(2,1)S(1)}, bf16[32,4096]{1,0:T(8,128)(2,1)S(1)}, u32[]{:S(2)}, u32[]{:S(2)}) collective-permute-start(bf16[32,4096]{1,0:T(8,128)(2,1)S(1)} %collective-permute-done), channel_id=1, source_target_pairs={{0,2},{1,3},{2,0},{3,1},{4,6},{5,7},{6,4},{7,5},{8,10},{9,11},{10,... | collective-permute-start | bytes 786440 | tf_op jit(solution)/shard_map/ppermute | solution.py:23
  15.5 7.3 %collective-permute-start.5 = (bf16[32,4096]{1,0:T(8,128)(2,1)S(1)}, bf16[32,4096]{1,0:T(8,128)(2,1)S(1)}, u32[]{:S(2)}, u32[]{:S(2)}) collective-permute-start(bf16[32,4096]{1,0:T(8,128)(2,1)S(1)} %collective-permute-done.1), channel_id=1, source_target_pairs={{0,2},{1,3},{2,0},{3,1},{4,6},{5,7},{6,4},{7,5},{8,10},{9,11},{10,... | collective-permute-start | bytes 786440 | tf_op jit(solution)/shard_map/ppermute | solution.py:23
  16.0 9.3 %collective-permute-start.7 = (bf16[32,4096]{1,0:T(8,128)(2,1)S(1)}, bf16[32,4096]{1,0:T(8,128)(2,1)S(1)}, u32[]{:S(2)}, u32[]{:S(2)}) collective-permute-start(bf16[32,4096]{1,0:T(8,128)(2,1)S(1)} %collective-permute-done.1), channel_id=1, source_target_pairs={{0,4},{1,5},{2,6},{3,7},{4,0},{5,1},{6,2},{7,3},{8,12},{9,13},{10,... | collective-permute-start | bytes 786440 | tf_op jit(solution)/shard_map/ppermute | solution.py:23
  25.4 2.4 %collective-permute-start.8 = (bf16[3,32,4096]{2,1,0:T(8,128)(2,1)S(1)}, bf16[3,32,4096]{2,1,0:T(8,128)(2,1)S(1)}, u32[]{:S(2)}, u32[]{:S(2)}) collective-permute-start(bf16[3,32,4096]{2,1,0:T(8,128)(2,1)S(1)} %pad_maximum_fusion.3), channel_id=1, source_target_pairs={{0,2},{1,3},{2,0},{3,1},{4,6},{5,7},{6,4},{7,5},{8,10},{9,11},{10,... | collective-permute-start | bytes 2359304 | tf_op jit(solution)/shard_map/ppermute | solution.py:23
